TPU v7x, 512 devices: a whole 4x4x16 slice. The times are simulated.
512 devices in a mesh: grp: 16 (over y, x), ctx: 32 (over z, core).
Axes of the slice: x: 4, y: 4, z: 16, core: 2. Of those that a mesh axis runs over, the one named last changes fastest.
Arguments:
- queries: bfloat16 [262144, 1024], P(('grp', 'ctx')), may hold values from -6 to 6
- keys: bfloat16 [262144, 1024], P(('grp', 'ctx')), may hold values from -6 to 6
- values: bfloat16 [262144, 1024], P(('grp', 'ctx')), may hold values from -6 to 6
- level_weights: float32 [13, 8, 262144], P(None, None, ('grp', 'ctx')), may hold values from 0.1 to 1.5
Outputs:
- attended: bfloat16 [262144, 1024], P(('grp', 'ctx'))
All inputs are finite; a program needn't handle non-finite values.
Results may differ from a plain program's by a relative error of at most 0.0095.
Values may be sent and summed in bfloat16 or wider, within the bound.
No kernel may reach another device: no remote copies, remote signals or barrier semaphores. Data moves between devices by JAX's collectives and lax.ppermute only.
A program may use at most 64 MiB of HBM per device.

v0:
```python
import math

import jax
import jax.numpy as jnp
from jax import lax
from jax.sharding import PartitionSpec as P

DK = 128
STRETCH = 64


def from_partner(block, axis, stride):
    count = lax.axis_size(axis)
    route = []
    for low in range(count):
        high = low | 1 << stride
        if high != low and high < count:
            route += [(low, high), (high, low)]
    return lax.ppermute(block, axis, route)


def level_factor(level_num):
    token_count = STRETCH if level_num == 0 else STRETCH * 2 ** (level_num - 1)
    return 1.0 / math.sqrt(DK * token_count)


def local_part(query_matrix, key_matrix, value_matrix, level_rows):
    row_count = query_matrix.shape[0]
    local_bits = (row_count // STRETCH).bit_length() - 1
    position = jnp.arange(row_count, dtype=jnp.int32)
    block_ids = position // STRETCH
    stretch_xor = jnp.bitwise_xor(block_ids[:, None], block_ids[None, :])
    level_ids = jnp.zeros((row_count, row_count), jnp.int32)
    for bit_num in range(local_bits):
        level_ids = level_ids + (stretch_xor >= 2**bit_num).astype(jnp.int32)
    causal = position[:, None] >= position[None, :]
    weight = jnp.zeros((level_rows.shape[1], row_count, row_count), jnp.float32)
    for level_num in range(local_bits + 1):
        picked = jnp.logical_and(level_ids == level_num, causal)
        weight = weight + jnp.where(
            picked[None], (level_rows[level_num] * level_factor(level_num))[:, :, None], 0.0
        )
    scores = jnp.einsum(
        "thk,shk->hts", query_matrix, key_matrix, preferred_element_type=jnp.float32
    )
    weighted = (scores * weight).astype(jnp.bfloat16)
    return jnp.einsum("hts,shv->thv", weighted, value_matrix, preferred_element_type=jnp.float32)


def sibling_weights(piece_rows, self_position, bit_count):
    device_ids = jnp.arange(piece_rows, dtype=jnp.int32)
    columns = []
    for bit_num in range(bit_count):
        own_block = jnp.right_shift(self_position, bit_num)
        member = jnp.logical_and(
            jnp.right_shift(device_ids, bit_num) == own_block - 1, own_block % 2 == 1
        )
        columns.append(member)
    return jnp.stack(columns, axis=1).astype(jnp.bfloat16)


def collect_into(self_position, bit_count, shard_rows):
    selector = sibling_weights(shard_rows.shape[0], self_position, bit_count)
    return jnp.einsum("nl,nhkv->lhkv", selector, shard_rows, preferred_element_type=jnp.float32)


def on_device(queries, keys, values, level_weights):
    row_count = queries.shape[0]
    head_count = level_weights.shape[1]
    head_width = queries.shape[1] // head_count
    query_matrix = queries.reshape(row_count, head_count, head_width)
    key_matrix = keys.reshape(row_count, head_count, head_width)
    value_matrix = values.reshape(row_count, head_count, head_width)
    local_bits = (row_count // STRETCH).bit_length() - 1
    ctx_bits = lax.axis_size("ctx").bit_length() - 1
    grp_bits = lax.axis_size("grp").bit_length() - 1
    ctx_index = lax.axis_index("ctx")
    grp_index = lax.axis_index("grp")
    kv_state = jnp.einsum(
        "pdx,pdo->dxo", key_matrix, value_matrix, preferred_element_type=jnp.float32
    ).astype(jnp.bfloat16)
    siblings = []
    running = kv_state.astype(jnp.float32)
    for bit_num in range(ctx_bits):
        partner = from_partner(running, "ctx", bit_num)
        left_half = jnp.right_shift(ctx_index, bit_num) % 2 == 1
        siblings.append(jnp.where(left_half, partner, 0.0))
        running = running + partner
    group_state = running.astype(jnp.bfloat16)
    summed = collect_into(
        grp_index, grp_bits, lax.all_gather(group_state[None], "grp", axis=0, tiled=True)
    )
    siblings.extend([summed[bit_num] for bit_num in range(grp_bits)])
    attended = local_part(query_matrix, key_matrix, value_matrix, level_weights)
    for bit_num in range(len(siblings)):
        level_num = 1 + local_bits + bit_num
        level_scale = (level_weights[level_num] * level_factor(level_num)).T
        outer_product = jnp.einsum(
            "ryl,ylf->ryf",
            query_matrix,
            siblings[bit_num].astype(jnp.bfloat16),
            preferred_element_type=jnp.float32,
        )
        attended = attended + outer_product * level_scale[:, :, None]
    return attended.reshape(row_count, head_count * head_width).astype(jnp.bfloat16)


def solution(mesh):
    return jax.shard_map(
        on_device,
        mesh=mesh,
        in_specs=(
            P(("grp", "ctx"), None),
            P(("grp", "ctx"), None),
            P(("grp", "ctx"), None),
            P(None, None, ("grp", "ctx")),
        ),
        out_specs=P(("grp", "ctx"), None),
        check_vma=False,
    )
```

profile of v0, /device:TPU:1, one launch (start us, length us, event | category | flops | bytes accessed | tf_op | source)
XLA Modules:
  0.0 256.2 jit_solution(629913876659027636)
XLA Ops:
  6.5 0.0 copy-start
  6.5 0.0 all-gather.3.cloned.1.call-start
  6.5 1.6 copy.118
  8.2 0.0 copy-done.14
  8.2 0.5 fusion.22
  8.7 8.7 %collective-permute-start = (f32[8,128,128]{2,1,0:T(8,128)S(1)}, f32[8,128,128]{2,1,0:T(8,128)S(1)}, u32[]{:S(2)}, u32[]{:S(2)}) collective-permute-start(f32[8,128,128]{2,1,0:T(8,128)S(1)} %fusion.22), channel_id=1, source_target_pairs={{0,1},{1,0},{2,3},{3,2},{4,5},{5,4},{6,7},{7,6},{8,9},{9,8},{10,11... | collective-permute-start | bytes 1572872 | tf_op jit(solution)/shard_map/ppermute | solution.py:19
  17.4 1.5 collective-permute-done
  18.9 0.1 add.144
  19.0 1.9 collective-permute-start.1
  20.9 0.0 copy-done.6
  21.0 13.1 %collective-permute-done.1 = f32[8,128,128]{2,1,0:T(8,128)S(1)} collective-permute-done((f32[8,128,128]{2,1,0:T(8,128)S(1)}, f32[8,128,128]{2,1,0:T(8,128)S(1)}, u32[]{:S(2)}, u32[]{:S(2)}) %collective-permute-start.1) | collective-permute-done | bytes 524320 | tf_op jit(solution)/shard_map/ppermute | solution.py:19
  34.0 0.1 add.147
  34.1 0.0 copy-start.15
  34.1 2.1 collective-permute-start.2
  36.2 25.9 %collective-permute-done.2 = f32[8,128,128]{2,1,0:T(8,128)S(1)} collective-permute-done((f32[8,128,128]{2,1,0:T(8,128)S(1)}, f32[8,128,128]{2,1,0:T(8,128)S(1)}, u32[]{:S(2)}, u32[]{:S(2)}) %collective-permute-start.2) | collective-permute-done | bytes 524320 | tf_op jit(solution)/shard_map/ppermute | solution.py:19
  62.1 0.1 add.150
  62.2 3.5 %collective-permute-start.3 = (f32[8,128,128]{2,1,0:T(8,128)S(1)}, f32[8,128,128]{2,1,0:T(8,128)S(1)}, u32[]{:S(2)}, u32[]{:S(2)}) collective-permute-start(f32[8,128,128]{2,1,0:T(8,128)S(1)} %add.150), channel_id=1, source_target_pairs={{0,8},{8,0},{1,9},{9,1},{2,10},{10,2},{3,11},{11,3},{4,12},{12,4},... | collective-permute-start | bytes 1572872 | tf_op jit(solution)/shard_map/ppermute | solution.py:19
  65.7 58.6 %collective-permute-done.3 = f32[8,128,128]{2,1,0:T(8,128)S(1)} collective-permute-done((f32[8,128,128]{2,1,0:T(8,128)S(1)}, f32[8,128,128]{2,1,0:T(8,128)S(1)}, u32[]{:S(2)}, u32[]{:S(2)}) %collective-permute-start.3) | collective-permute-done | bytes 524320 | tf_op jit(solution)/shard_map/ppermute | solution.py:19
  124.2 0.1 add.153
  124.3 0.0 copy-done.7
  124.3 10.8 %collective-permute-start.4 = (f32[8,128,128]{2,1,0:T(8,128)S(1)}, f32[8,128,128]{2,1,0:T(8,128)S(1)}, u32[]{:S(2)}, u32[]{:S(2)}) collective-permute-start(f32[8,128,128]{2,1,0:T(8,128)S(1)} %add.153), channel_id=1, source_target_pairs={{0,16},{16,0},{1,17},{17,1},{2,18},{18,2},{3,19},{19,3},{4,20},{20... | collective-permute-start | bytes 1572872 | tf_op jit(solution)/shard_map/ppermute | solution.py:19
  135.1 17.5 %collective-permute-done.4 = f32[8,128,128]{2,1,0:T(8,128)S(1)} collective-permute-done((f32[8,128,128]{2,1,0:T(8,128)S(1)}, f32[8,128,128]{2,1,0:T(8,128)S(1)}, u32[]{:S(2)}, u32[]{:S(2)}) %collective-permute-start.4) | collective-permute-done | bytes 524320 | tf_op jit(solution)/shard_map/ppermute | solution.py:19
  152.6 0.0 copy-done.9
  152.6 0.0 copy-done.11
  152.6 0.8 copy-done.4
  153.5 0.8 add_convert_fusion
  154.2 0.0 all-gather.3.cloned.1.call-update
  154.3 0.6 compare_and_fusion
  154.9 0.6 compare_and_fusion.2
  155.5 0.0 copy-done.15
  155.5 0.6 multiply_bitcast_fusion.8
  156.2 1.8 fusion.47
  157.9 0.0 copy-done
  157.9 7.6 %fusion.2 = f32[8,512,128]{1,2,0:T(8,128)} fusion(f32[8,512]{1,0:T(8,128)} %get-tuple-element.16, f32[8,512]{1,0:T(8,128)} %get-tuple-element.17, f32[8,512]{1,0:T(8,128)} %get-tuple-element.18, f32[8,512]{1,0:T(8,128)} %get-tuple-element.19, pred[512,512]{1,0:T(8,128)(4,1)} %get-tuple-element.23, pred[512,512]{1,0:T(8,128)(4,1)} %get-tuple-element.25, ...), kind=kOutput, calls=%fused_computation.3 | convolution fusion | flops 1092616192 | bytes 6356992 | tf_op jit(solution)/shard_map/hts,shv->thv/dot_general | solution.py:47
  165.6 1.6 fusion.40
  167.1 0.0 copy-done.8
  167.2 0.0 copy-start.10
  167.2 1.9 fusion.38
  169.1 0.0 copy-done.10
  169.1 1.9 fusion.36
  170.9 0.0 copy-done.12
  170.9 0.0 copy-start.19
  170.9 1.9 fusion.34
  172.8 60.0 %all-gather.3.cloned.1.call-done = bf16[128,128,128]{2,1,0:T(8,128)(2,1)} async-done(((bf16[8,128,128]{2,1,0:T(8,128)(2,1)}), bf16[128,128,128]{2,1,0:T(8,128)(2,1)}) %all-gather.3.cloned.1.call-update) | async-done | bytes 4194320 | tf_op jit(solution)/shard_map/all_gather | solution.py:91
  232.8 0.0 copy-done.16
  232.8 0.0 copy-done.17
  232.8 0.0 copy-done.18
  232.8 0.0 copy-done.19
  232.8 4.8 %fusion.19 = bf16[4,8,128,128]{3,0,2,1:T(4,128)(2,1)S(1)} fusion(bf16[16,8,128,128]{3,2,1,0:T(8,128)(2,1)} %bitcast.192, pred[16,1]{0,1:T(4,128)(4,1)S(1)} %copy-done.16, pred[16,1]{0,1:T(4,128)(4,1)S(1)} %copy-done.17, pred[16,1]{0,1:T(4,128)(4,1)S(1)} %copy-done.18, pred[16,1]{0,1:T(4,128)(4,1)S(1)} %copy-done.19), kind=kOutput, calls=%fused_computation.31 | convolution fusion | flops 17301696 | bytes 5242944 | tf_op jit(solution)/shard_map/nl,nhkv->lhkv/dot_general | solution.py:64
  237.5 2.2 fusion.99
  239.7 0.5 fusion.31
  240.2 0.0 copy-start.13
  240.2 0.5 fusion.25
  240.7 0.0 copy-start.2
  240.7 0.0 copy-start.3
  240.7 0.5 fusion.27
  241.2 0.5 fusion.29
  241.7 0.1 copy-done.13
  241.8 0.8 copy-done.2
  242.5 0.6 copy-done.3
  243.2 0.7 copy-done.1
  243.9 0.0 copy-done.5
  243.9 3.2 %fusion.10 = bf16[512,8,128]{0,2,1:T(8,128)(2,1)} fusion(f32[8,128,512]{2,1,0:T(8,128)S(1)} %fusion.25, f32[8,128,512]{2,1,0:T(8,128)S(1)} %fusion.27, f32[8,128,512]{2,1,0:T(8,128)S(1)} %fusion.29, f32[8,128,512]{2,1,0:T(8,128)S(1)} %fusion.31, f32[8,128,512]{2,1,0:T(8,128)S(1)} %copy-done.3, f32[8,128,512]{2,1,0:T(8,128)S(1)} %copy-done.2, ...), kind=kOutput, calls=%fused_computation.11 | convolution fusion | flops 144310272 | bytes 21643264 | tf_op jit(solution)/shard_map/ryl,ylf->ryf/dot_general | solution.py:98
  247.1 2.3 copy.99
  (14 shorter events, 0.0 us)
Async XLA Ops:
  6.5 151.4 %copy-start = (bf16[512,1024]{1,0:T(8,128)(2,1)S(1)}, bf16[512,1024]{1,0:T(8,128)(2,1)}, u32[]{:S(2)}) copy-start(bf16[512,1024]{1,0:T(8,128)(2,1)} %param.4) | copy-start | bytes 3145732
  6.5 1.7 copy-start.14
  6.5 226.2 %all-gather.3.cloned.1.call-start = ((), (), s32[]{:S(2)}) async-start(), calls=%async_computation | async-start | bytes 4456448 | tf_op jit(solution)/shard_map/all_gather | solution.py:91
  8.7 10.3 %collective-permute-start = (f32[8,128,128]{2,1,0:T(8,128)S(1)}, f32[8,128,128]{2,1,0:T(8,128)S(1)}, u32[]{:S(2)}, u32[]{:S(2)}) collective-permute-start(f32[8,128,128]{2,1,0:T(8,128)S(1)} %fusion.22), channel_id=1, source_target_pairs={{0,1},{1,0},{2,3},{3,2},{4,5},{5,4},{6,7},{7,6},{8,9},{9,8},{10,11... | collective-permute-start | bytes 1572872 | tf_op jit(solution)/shard_map/ppermute | solution.py:19
  18.9 2.0 copy-start.6
  19.0 15.0 %collective-permute-start.1 = (f32[8,128,128]{2,1,0:T(8,128)S(1)}, f32[8,128,128]{2,1,0:T(8,128)S(1)}, u32[]{:S(2)}, u32[]{:S(2)}) collective-permute-start(f32[8,128,128]{2,1,0:T(8,128)S(1)} %add.144), channel_id=1, source_target_pairs={{0,2},{2,0},{1,3},{3,1},{4,6},{6,4},{5,7},{7,5},{8,10},{10,8},{9,1... | collective-permute-start | bytes 1572872 | tf_op jit(solution)/shard_map/ppermute | solution.py:19
  34.0 90.3 %copy-start.7 = (f32[8,128,128]{2,1,0:T(8,128)}, f32[8,128,128]{2,1,0:T(8,128)S(1)}, u32[]{:S(2)}) copy-start(f32[8,128,128]{2,1,0:T(8,128)S(1)} %collective-permute-done.1) | copy-start | bytes 1572868
  34.1 121.4 %copy-start.15 = (f32[13,8,512]{2,1,0:T(8,128)S(1)}, f32[13,8,512]{2,1,0:T(8,128)}, u32[]{:S(2)}) copy-start(f32[13,8,512]{2,1,0:T(8,128)} %param.7) | copy-start | bytes 638980
  34.1 28.0 %collective-permute-start.2 = (f32[8,128,128]{2,1,0:T(8,128)S(1)}, f32[8,128,128]{2,1,0:T(8,128)S(1)}, u32[]{:S(2)}, u32[]{:S(2)}) collective-permute-start(f32[8,128,128]{2,1,0:T(8,128)S(1)} %add.147), channel_id=1, source_target_pairs={{0,4},{4,0},{1,5},{5,1},{2,6},{6,2},{3,7},{7,3},{8,12},{12,8},{9,1... | collective-permute-start | bytes 1572872 | tf_op jit(solution)/shard_map/ppermute | solution.py:19
  62.1 90.5 %copy-start.9 = (f32[8,128,128]{2,1,0:T(8,128)}, f32[8,128,128]{2,1,0:T(8,128)S(1)}, u32[]{:S(2)}) copy-start(f32[8,128,128]{2,1,0:T(8,128)S(1)} %collective-permute-done.2) | copy-start | bytes 1572868
  62.2 62.1 %collective-permute-start.3 = (f32[8,128,128]{2,1,0:T(8,128)S(1)}, f32[8,128,128]{2,1,0:T(8,128)S(1)}, u32[]{:S(2)}, u32[]{:S(2)}) collective-permute-start(f32[8,128,128]{2,1,0:T(8,128)S(1)} %add.150), channel_id=1, source_target_pairs={{0,8},{8,0},{1,9},{9,1},{2,10},{10,2},{3,11},{11,3},{4,12},{12,4},... | collective-permute-start | bytes 1572872 | tf_op jit(solution)/shard_map/ppermute | solution.py:19
  124.2 28.4 %copy-start.11 = (f32[8,128,128]{2,1,0:T(8,128)}, f32[8,128,128]{2,1,0:T(8,128)S(1)}, u32[]{:S(2)}) copy-start(f32[8,128,128]{2,1,0:T(8,128)S(1)} %collective-permute-done.3) | copy-start | bytes 1572868
  124.3 28.3 %collective-permute-start.4 = (f32[8,128,128]{2,1,0:T(8,128)S(1)}, f32[8,128,128]{2,1,0:T(8,128)S(1)}, u32[]{:S(2)}, u32[]{:S(2)}) collective-permute-start(f32[8,128,128]{2,1,0:T(8,128)S(1)} %add.153), channel_id=1, source_target_pairs={{0,16},{16,0},{1,17},{17,1},{2,18},{18,2},{3,19},{19,3},{4,20},{20... | collective-permute-start | bytes 1572872 | tf_op jit(solution)/shard_map/ppermute | solution.py:19
  152.6 0.8 copy-start.4
  165.6 1.6 copy-start.8
  167.2 1.9 copy-start.10
  169.1 1.9 copy-start.12
  170.9 61.8 %copy-start.16 = (pred[16,1]{0,1:T(4,128)(4,1)S(1)}, pred[16,1]{0,1:T(4,128)(4,1)}, u32[]{:S(2)}) copy-start(pred[16,1]{0,1:T(4,128)(4,1)} %get-tuple-element.26) | copy-start | bytes 52
  170.9 61.8 %copy-start.17 = (pred[16,1]{0,1:T(4,128)(4,1)S(1)}, pred[16,1]{0,1:T(4,128)(4,1)}, u32[]{:S(2)}) copy-start(pred[16,1]{0,1:T(4,128)(4,1)} %get-tuple-element.27) | copy-start | bytes 52
  170.9 61.8 %copy-start.18 = (pred[16,1]{0,1:T(4,128)(4,1)S(1)}, pred[16,1]{0,1:T(4,128)(4,1)}, u32[]{:S(2)}) copy-start(pred[16,1]{0,1:T(4,128)(4,1)} %get-tuple-element.28) | copy-start | bytes 52
  170.9 61.8 %copy-start.19 = (pred[16,1]{0,1:T(4,128)(4,1)S(1)}, pred[16,1]{0,1:T(4,128)(4,1)}, u32[]{:S(2)}) copy-start(pred[16,1]{0,1:T(4,128)(4,1)} %get-tuple-element.29) | copy-start | bytes 52
  240.2 1.6 copy-start.13
  240.7 1.8 copy-start.2
  240.7 2.5 copy-start.3
  241.2 2.7 %copy-start.1 = (f32[8,128,512]{2,1,0:T(8,128)S(1)}, f32[8,128,512]{2,1,0:T(8,128)}, u32[]{:S(2)}) copy-start(f32[8,128,512]{2,1,0:T(8,128)} %fusion.38) | copy-start | bytes 6291460
  241.2 2.7 %copy-start.5 = (f32[8,128,128]{2,1,0:T(8,128)S(1)}, f32[8,128,128]{2,1,0:T(8,128)}, u32[]{:S(2)}) copy-start(f32[8,128,128]{2,1,0:T(8,128)} %copy-done.4) | copy-start | bytes 1572868
Sparse Core Ops, SparseCore 0:
  154.4 78.3 all-gather.2
where the time goes:
time: 257 us; the launch traced here: 256 us
  waiting for transfers between devices  177 us (69%)
  starting transfers between devices  27 us (11%)
  matrix products  25.2 us (10%)
  between operations  13.7 us (5%)
  local copies, waits for them, and re-layouts  9.12 us (4%)
  other arithmetic  4.59 us (2%)
    ppermute x5, waiting for transfers between devices, from_partner(): return lax.ppermute(block, axis, route)  117 us
    all_gather x1, waiting for transfers between devices, on_device(): lax.all_gather(group_state[None], 'grp', axis=0, tiled=True)  60 us
    ppermute x5, starting transfers between devices, from_partner(): return lax.ppermute(block, axis, route)  27 us
    dot_general x9, matrix products, on_device(): jnp.einsum('ryl,ylf->ryf', query_matrix, siblings[bit_num].astype(jnp.bfl...  12.3 us
    dot_general x1, matrix products, local_part(): jnp.einsum('hts,shv->thv', weighted, value_matrix, preferred_element_type...  7.63 us
  transfers between devices with their start and end apart: 6, of which 6 were waited for; matrix products, arithmetic and copies ran while one was open for 7% of the time, Pallas kernels for 0%

commit v1 on v0

v1 whole, which is shorter than its diff:
```python
import functools
import math

import jax
import jax.numpy as jnp
from jax import lax
from jax.experimental import pallas as pl
from jax.experimental.pallas import tpu as pltpu
from jax.sharding import PartitionSpec as P

DK = 128
STRETCH = 64
F32 = jnp.float32
BF16 = jnp.bfloat16


def level_factor(level_num):
    token_count = STRETCH if level_num == 0 else STRETCH * 2 ** (level_num - 1)
    return 1.0 / math.sqrt(DK * token_count)


def swap(block, axis, stride):
    count = lax.axis_size(axis)
    return lax.ppermute(block, axis, [(i, i ^ stride) for i in range(count)])


def on_chip(x):
    return pltpu.with_memory_space_constraint(x, pltpu.VMEM)


def state_kernel(half_ref, k_ref, v_ref, o_ref):
    o_ref[0] = lax.dot_general(
        k_ref[...], v_ref[...], (((0,), (0,)), ((), ())), preferred_element_type=F32
    ).astype(BF16)


def half_state(half, keys, values):
    rows, width = keys.shape
    heads = width // DK // 2
    spec = pl.BlockSpec((rows, DK), lambda i, h: (0, h[0] * heads + i))
    return pl.pallas_call(
        state_kernel,
        out_shape=jax.ShapeDtypeStruct((heads, DK, DK), BF16),
        grid_spec=pltpu.PrefetchScalarGridSpec(
            num_scalar_prefetch=1,
            grid=(heads,),
            in_specs=[spec, spec],
            out_specs=pl.BlockSpec((1, DK, DK), lambda i, h: (i, 0, 0)),
        ),
        cost_estimate=pl.CostEstimate(
            flops=2 * rows * DK * DK * heads, transcendentals=0, bytes_accessed=4 * rows * DK * heads
        ),
        name="half_state",
    )(half, keys, values)


def local_kernel(q_ref, k_ref, v_ref, s_ref, o_ref):
    rows = q_ref.shape[0]
    tile = 2 * STRETCH
    scale = s_ref[0].T
    row = lax.broadcasted_iota(jnp.int32, (tile, tile), 0)
    col = lax.broadcasted_iota(jnp.int32, (tile, tile), 1)
    low = jnp.logical_and(row >= STRETCH, col < STRETCH)
    same = jnp.logical_and(col <= row, jnp.logical_not(low))
    for r in range(rows // tile):
        at = pl.ds(r * tile, tile)
        query = q_ref[at, :]
        pick = scale[r * tile : (r + 1) * tile]
        span = (r + 1) * tile
        score = lax.dot_general(
            query, k_ref[pl.ds(0, span), :], (((1,), (1,)), ((), ())), preferred_element_type=F32
        )
        parts = []
        for c in range(r):
            level = 1 + (r ^ c).bit_length()
            parts.append(score[:, c * tile : (c + 1) * tile] * pick[:, level : level + 1])
        weight = jnp.where(same, pick[:, 0:1], jnp.where(low, pick[:, 1:2], 0.0))
        parts.append(score[:, r * tile :] * weight)
        weighted = jnp.concatenate([p.astype(BF16) for p in parts], axis=1)
        o_ref[at, :] = jnp.dot(weighted, v_ref[pl.ds(0, span), :], preferred_element_type=F32)


def local_part(queries, keys, values, scales):
    rows, width = queries.shape
    heads = width // DK
    spec = pl.BlockSpec((rows, DK), lambda h: (0, h))
    return pl.pallas_call(
        local_kernel,
        out_shape=jax.ShapeDtypeStruct((rows, width), F32),
        grid=(heads,),
        in_specs=[spec, spec, spec, pl.BlockSpec((1,) + scales.shape[1:], lambda h: (h, 0, 0))],
        out_specs=spec,
        cost_estimate=pl.CostEstimate(
            flops=4 * rows * rows * width, transcendentals=0, bytes_accessed=10 * rows * width
        ),
        name="local_part",
    )(queries, keys, values, scales)


def gather_kernel(bits, place_ref, first_ref, other_ref, *refs):
    ctx_refs, (all_ref, o_ref) = refs[:-2], refs[-2:]
    own = place_ref[0]
    o_ref[0] = jnp.where(place_ref[1] == 1, first_ref[...], other_ref[...])
    for b, ctx_ref in enumerate(ctx_refs):
        o_ref[1 + b] = ctx_ref[...]
    for b in range(bits):
        low = jnp.maximum(lax.shift_right_logical(own, b) - 1, 0) * 2**b
        for h in range(o_ref.shape[1]):
            total = all_ref[low, h].astype(F32)
            for i in range(1, 2**b):
                total = total + all_ref[low + i, h].astype(F32)
            o_ref[1 + len(ctx_refs) + b, h] = total.astype(BF16)


def gather_levels(place, first, other, ctx_levels, group_states):
    runs, heads = group_states.shape[:2]
    bits = runs.bit_length() - 1
    levels = 1 + len(ctx_levels) + bits
    return pl.pallas_call(
        functools.partial(gather_kernel, bits),
        out_shape=jax.ShapeDtypeStruct((levels, heads, DK, DK), BF16),
        in_specs=[pl.BlockSpec(memory_space=pltpu.SMEM)]
        + [pl.BlockSpec(memory_space=pltpu.VMEM)] * (3 + len(ctx_levels)),
        out_specs=pl.BlockSpec(memory_space=pltpu.VMEM),
        compiler_params=pltpu.CompilerParams(vmem_limit_bytes=16 << 20),
        name="gather_levels",
    )(place, first, other, *ctx_levels, on_chip(group_states))


def final_kernel(first_level, place_ref, q_ref, a_ref, s_ref, mine_ref, their_ref, o_ref):
    levels, half = mine_ref.shape[:2]
    for i in range(2 * half):
        states, n = (mine_ref, i) if i < half else (their_ref, i - half)
        side = place_ref[1] if i < half else 1 - place_ref[1]
        head = side * half + n
        at = pl.ds(pl.multiple_of(head * DK, DK), DK)
        scale = s_ref[head].T
        query = q_ref[:, at]
        total = a_ref[:, at]
        for j in range(levels):
            part = jnp.dot(query, states[j, n], preferred_element_type=F32)
            total = total + part * scale[:, first_level + j : first_level + j + 1]
        o_ref[:, at] = total.astype(BF16)


def final_part(place, queries, local, scales, mine, theirs, first_level):
    rows, width = queries.shape
    return pl.pallas_call(
        functools.partial(final_kernel, first_level),
        out_shape=jax.ShapeDtypeStruct((rows, width), BF16),
        in_specs=[pl.BlockSpec(memory_space=pltpu.SMEM)] + [pl.BlockSpec(memory_space=pltpu.VMEM)] * 5,
        out_specs=pl.BlockSpec(memory_space=pltpu.VMEM),
        compiler_params=pltpu.CompilerParams(vmem_limit_bytes=32 << 20),
        name="final_part",
    )(place, queries, local, scales, on_chip(mine), on_chip(theirs))


def on_device(queries, keys, values, level_weights):
    rows = queries.shape[0]
    local_bits = (rows // STRETCH).bit_length() - 1
    ctx_bits = lax.axis_size("ctx").bit_length() - 1
    grp_bits = lax.axis_size("grp").bit_length() - 1
    runs = lax.axis_size("grp")
    ctx_index = lax.axis_index("ctx").astype(jnp.int32)
    grp_index = lax.axis_index("grp").astype(jnp.int32)
    core = ctx_index % 2
    place = jnp.stack([grp_index, core])

    block = grp_index * lax.axis_size("ctx") + ctx_index
    level_ids = jnp.arange(level_weights.shape[0], dtype=jnp.int32)
    bit_of = jnp.maximum(level_ids - 1 - local_bits, 0)
    live = jnp.logical_or(level_ids <= local_bits, jnp.right_shift(block, bit_of) % 2 == 1)
    factor = jnp.asarray([level_factor(n) for n in range(level_weights.shape[0])], F32)
    gain = jnp.where(live, factor, 0.0)
    scales = jnp.transpose(level_weights * gain[:, None, None], (1, 0, 2))
    scales = jnp.pad(scales, ((0, 0), (0, -scales.shape[1] % 8), (0, 0)))

    send = half_state((1 - core)[None], keys, values)
    first = swap(send, "ctx", 1)
    keep = half_state(core[None], keys, values)
    running = keep.astype(F32) + first.astype(F32)
    ctx_levels = []
    for b in range(1, ctx_bits):
        partner = swap(running.astype(BF16), "ctx", 1 << b)
        ctx_levels.append(partner)
        running = running + partner.astype(F32)
    total = running.astype(BF16)
    group_states = lax.all_to_all(
        jnp.broadcast_to(total[None], (runs,) + total.shape), "grp", 0, 0, tiled=True
    )
    local = local_part(queries, keys, values, scales)
    group_states, local = lax.optimization_barrier((group_states, local))
    mine = gather_levels(place, first, keep, ctx_levels, group_states)
    theirs = swap(mine, "ctx", 1)
    return final_part(place, queries, local, scales, mine, theirs, 1 + local_bits)


def solution(mesh):
    return jax.shard_map(
        on_device,
        mesh=mesh,
        in_specs=(
            P(("grp", "ctx"), None),
            P(("grp", "ctx"), None),
            P(("grp", "ctx"), None),
            P(None, None, ("grp", "ctx")),
        ),
        out_specs=P(("grp", "ctx"), None),
        check_vma=False,
    )
```

time: 257 us -> 135 us (0.53)
  waiting for transfers between devices: 177 us -> 62.4 us
  matrix products: 25.2 us -> 0 us
  Pallas kernels: 0 us -> 25.2 us
  between operations: 13.7 us -> 0.14 us
  starting transfers between devices: 27 us -> 36.6 us
  local copies, waits for them, and re-layouts: 9.12 us -> 5.29 us
    ppermute x5 -> x6, waiting for transfers between devices: 117 us -> 43.4 us  [swap(): return lax.ppermute(block, axis, [(i, i ^ stride) for i in range(count)])]
    all_gather x1 -> x0, waiting for transfers between devices: 60 us -> none  [on_device(): lax.all_gather(group_state[None], 'grp', axis=0, tiled=True)]
    pallas_call x0 -> x5, Pallas kernels: none -> 25.2 us  [the longest x1 9.63 us: local_part(): pl.pallas_call(local_kernel, out_shape=jax.ShapeDtypeStruct((rows, width)...]
    dot_general x12 -> x0, matrix products: 25.2 us -> none  [the longest x9 12.3 us: on_device(): jnp.einsum('ryl,ylf->ryf', query_matrix, siblings[bit_num].astype(jnp.bfl...]
    all_to_all x0 -> x1, waiting for transfers between devices: none -> 19 us  [on_device(): lax.all_to_all(jnp.broadcast_to(total[None], (runs,) + total.shape), 'grp...]
    all_to_all x0 -> x1, starting transfers between devices: none -> 5.1 us  [on_device(): lax.all_to_all(jnp.broadcast_to(total[None], (runs,) + total.shape), 'grp...]
    ppermute x5 -> x6, starting transfers between devices: 27 us -> 31.5 us  [swap(): return lax.ppermute(block, axis, [(i, i ^ stride) for i in range(count)])]
    convert_element_type x1 -> x5, other arithmetic: 0.76 us -> 4.14 us  [the longest x4 4.03 us: on_device(): partner = swap(running.astype(BF16), 'ctx', 1 << b)]
  transfers between devices with their start and end apart: 6 -> 7, of which waited for: 6 -> 6; matrix products, arithmetic and copies ran while one was open for 7% -> 1% of each run, Pallas kernels for 0% -> 10%
where the time goes in v1:
time: 135 us; the launch traced here: 134 us
  waiting for transfers between devices  62.4 us (46%)
  starting transfers between devices  36.6 us (27%)
  Pallas kernels  25.2 us (19%)
  local copies, waits for them, and re-layouts  5.29 us (4%)
  other arithmetic  4.36 us (3%)
    ppermute x6, waiting for transfers between devices, swap(): return lax.ppermute(block, axis, [(i, i ^ stride) for i in range(count)])  43.4 us
    ppermute x6, starting transfers between devices, swap(): return lax.ppermute(block, axis, [(i, i ^ stride) for i in range(count)])  31.5 us
    all_to_all x1, waiting for transfers between devices, on_device(): lax.all_to_all(jnp.broadcast_to(total[None], (runs,) + total.shape), 'grp...  19 us
    pallas_call x1, Pallas kernels, local_part(): pl.pallas_call(local_kernel, out_shape=jax.ShapeDtypeStruct((rows, width)...  9.63 us
    pallas_call x1, Pallas kernels, final_part(): pl.pallas_call(functools.partial(final_kernel, first_level), out_shape=ja...  7.39 us
    pallas_call x2, Pallas kernels, half_state(): pl.pallas_call(state_kernel, out_shape=jax.ShapeDtypeStruct((heads, DK, D...  7.33 us
    all_to_all x1, starting transfers between devices, on_device(): lax.all_to_all(jnp.broadcast_to(total[None], (runs,) + total.shape), 'grp...  5.1 us
    convert_element_type x4, other arithmetic, on_device(): partner = swap(running.astype(BF16), 'ctx', 1 << b)  4.03 us
  transfers between devices with their start and end apart: 7, of which 6 were waited for; matrix products, arithmetic and copies ran while one was open for 1% of the time, Pallas kernels for 10%

profile of v1, /device:TPU:1, one launch (start us, length us, event | category | flops | bytes accessed | tf_op | source)
XLA Modules:
  0.0 134.0 jit_solution(17640680525598426006)
XLA Ops:
  0.0 3.7 %half_state.3 = bf16[4,128,128]{2,1,0:T(8,128)(2,1)} custom-call(s32[1]{0:T(128)} %bitcast.2.half_ref, bf16[512,1024]{1,0:T(8,128)(2,1)} %k_ref.5, bf16[512,1024]{1,0:T(8,128)(2,1)} %v_ref.5), custom_call_target="tpu_custom_call" | custom-call | flops 67108864 | bytes 1048576 | tf_op jit(solution)/shard_map/half_state/pallas_call | solution.py:41
  3.7 8.7 %collective-permute-start = (bf16[4,128,128]{2,1,0:T(8,128)(2,1)}, bf16[4,128,128]{2,1,0:T(8,128)(2,1)S(1)}, u32[]{:S(2)}, u32[]{:S(2)}) collective-permute-start(bf16[4,128,128]{2,1,0:T(8,128)(2,1)} %half_state.3), channel_id=1, source_target_pairs={{0,1},{1,0},{2,3},{3,2},{4,5},{5,4},{6,7},{7,6},{8,9},{9,8},{10,11... | collective-permute-start | bytes 393224 | tf_op jit(solution)/shard_map/ppermute | solution.py:24
  12.4 3.7 %half_state.2.other_ref = bf16[4,128,128]{2,1,0:T(8,128)(2,1)} custom-call(s32[1]{0:T(128)} %bitcast.1.half_ref, bf16[512,1024]{1,0:T(8,128)(2,1)} %k_ref.5, bf16[512,1024]{1,0:T(8,128)(2,1)} %v_ref.5), custom_call_target="tpu_custom_call" | custom-call | flops 67108864 | bytes 1048576 | tf_op jit(solution)/shard_map/half_state/pallas_call | solution.py:41
  16.1 0.0 copy-start.1
  16.1 0.0 collective-permute-done.first_ref
  16.1 1.0 fusion.1
  17.1 1.9 %collective-permute-start.1 = (bf16[4,128,128]{2,1,0:T(8,128)(2,1)S(1)}, bf16[4,128,128]{2,1,0:T(8,128)(2,1)S(1)}, u32[]{:S(2)}, u32[]{:S(2)}) collective-permute-start(bf16[4,128,128]{2,1,0:T(8,128)(2,1)S(1)} %fusion.1), channel_id=1, source_target_pairs={{0,2},{1,3},{2,0},{3,1},{4,6},{5,7},{6,4},{7,5},{8,10},{9,11},{10,... | collective-permute-start | bytes 393224 | tf_op jit(solution)/shard_map/ppermute | solution.py:24
  19.0 5.0 %collective-permute-done.1.refs_0_ = bf16[4,128,128]{2,1,0:T(8,128)(2,1)S(1)} collective-permute-done((bf16[4,128,128]{2,1,0:T(8,128)(2,1)S(1)}, bf16[4,128,128]{2,1,0:T(8,128)(2,1)S(1)}, u32[]{:S(2)}, u32[]{:S(2)}) %collective-permute-start.1) | collective-permute-done | bytes 131104 | tf_op jit(solution)/shard_map/ppermute | solution.py:24
  24.0 1.0 fusion.5
  25.0 1.9 %collective-permute-start.2 = (bf16[4,128,128]{2,1,0:T(8,128)(2,1)S(1)}, bf16[4,128,128]{2,1,0:T(8,128)(2,1)S(1)}, u32[]{:S(2)}, u32[]{:S(2)}) collective-permute-start(bf16[4,128,128]{2,1,0:T(8,128)(2,1)S(1)} %fusion.5), channel_id=1, source_target_pairs={{0,4},{1,5},{2,6},{3,7},{4,0},{5,1},{6,2},{7,3},{8,12},{9,13},{10,... | collective-permute-start | bytes 393224 | tf_op jit(solution)/shard_map/ppermute | solution.py:24
  26.9 9.1 %collective-permute-done.2.refs_1_ = bf16[4,128,128]{2,1,0:T(8,128)(2,1)S(1)} collective-permute-done((bf16[4,128,128]{2,1,0:T(8,128)(2,1)S(1)}, bf16[4,128,128]{2,1,0:T(8,128)(2,1)S(1)}, u32[]{:S(2)}, u32[]{:S(2)}) %collective-permute-start.2) | collective-permute-done | bytes 131104 | tf_op jit(solution)/shard_map/ppermute | solution.py:24
  36.0 0.0 copy-start.4
  36.0 1.0 fusion.2
  37.0 3.7 %collective-permute-start.3 = (bf16[4,128,128]{2,1,0:T(8,128)(2,1)S(1)}, bf16[4,128,128]{2,1,0:T(8,128)(2,1)S(1)}, u32[]{:S(2)}, u32[]{:S(2)}) collective-permute-start(bf16[4,128,128]{2,1,0:T(8,128)(2,1)S(1)} %fusion.2), channel_id=1, source_target_pairs={{0,8},{1,9},{2,10},{3,11},{4,12},{5,13},{6,14},{7,15},{8,0},{9,1},... | collective-permute-start | bytes 393224 | tf_op jit(solution)/shard_map/ppermute | solution.py:24
  40.8 13.3 %collective-permute-done.3.refs_2_ = bf16[4,128,128]{2,1,0:T(8,128)(2,1)S(1)} collective-permute-done((bf16[4,128,128]{2,1,0:T(8,128)(2,1)S(1)}, bf16[4,128,128]{2,1,0:T(8,128)(2,1)S(1)}, u32[]{:S(2)}, u32[]{:S(2)}) %collective-permute-start.3) | collective-permute-done | bytes 131104 | tf_op jit(solution)/shard_map/ppermute | solution.py:24
  54.1 0.0 copy-start.6
  54.1 1.0 fusion.3
  55.1 10.8 %collective-permute-start.4 = (bf16[4,128,128]{2,1,0:T(8,128)(2,1)S(1)}, bf16[4,128,128]{2,1,0:T(8,128)(2,1)S(1)}, u32[]{:S(2)}, u32[]{:S(2)}) collective-permute-start(bf16[4,128,128]{2,1,0:T(8,128)(2,1)S(1)} %fusion.3), channel_id=1, source_target_pairs={{0,16},{1,17},{2,18},{3,19},{4,20},{5,21},{6,22},{7,23},{8,24},{9,... | collective-permute-start | bytes 393224 | tf_op jit(solution)/shard_map/ppermute | solution.py:24
  65.9 13.6 %collective-permute-done.4.refs_3_ = bf16[4,128,128]{2,1,0:T(8,128)(2,1)S(1)} collective-permute-done((bf16[4,128,128]{2,1,0:T(8,128)(2,1)S(1)}, bf16[4,128,128]{2,1,0:T(8,128)(2,1)S(1)}, u32[]{:S(2)}, u32[]{:S(2)}) %collective-permute-start.4) | collective-permute-done | bytes 131104 | tf_op jit(solution)/shard_map/ppermute | solution.py:24
  79.5 0.0 copy-done.1
  79.5 0.0 copy-start.8
  79.5 0.1 add_convert_fusion
  79.7 1.8 %broadcast_in_dim.16 = bf16[16,4,128,128]{3,2,1,0:T(8,128)(2,1)} broadcast(bf16[4,128,128]{2,1,0:T(8,128)(2,1)S(1)} %add_convert_fusion), dimensions={1,2,3} | broadcast | bytes 2228224 | tf_op jit(solution)/shard_map/broadcast_in_dim | solution.py:189
  81.5 0.0 copy-done.4
  81.5 0.0 copy-start.11
  81.5 0.0 copy-start.10
  81.5 0.0 copy-done.6
  81.5 0.0 copy-done.8
  81.5 5.1 %all-to-all-start = ((bf16[16,4,128,128]{3,2,1,0:T(8,128)(2,1)}), bf16[16,4,128,128]{3,2,1,0:T(8,128)(2,1)S(1)}, u32[]{:S(2)}, u32[]{:S(2)}) async-start(bf16[16,4,128,128]{3,2,1,0:T(8,128)(2,1)} %broadcast_in_dim.16), calls=%async_computation | async-start | bytes 4194304 | tf_op jit(solution)/shard_map/all_to_all | solution.py:188
  86.6 0.0 copy-done.11
  86.6 0.0 copy-done.10
  86.7 0.1 fusion
  86.8 0.7 pad.4.s_ref
  87.5 9.6 %local_part.1.a_ref = f32[512,1024]{1,0:T(8,128)} custom-call(bf16[512,1024]{1,0:T(8,128)(2,1)} %q_ref.3, bf16[512,1024]{1,0:T(8,128)(2,1)} %k_ref.5, bf16[512,1024]{1,0:T(8,128)(2,1)} %v_ref.5, f32[8,16,512]{2,1,0:T(8,128)} %pad.4.s_ref), custom_call_target="tpu_custom_call" | custom-call | flops 1073741824 | bytes 5242880 | tf_op jit(solution)/shard_map/local_part/pallas_call | solution.py:87
  97.1 0.0 copy-start.2
  97.2 0.1 pad_add_fusion.place_ref
  97.2 19.0 %all-to-all-done.refs_4_ = bf16[16,4,128,128]{3,2,1,0:T(8,128)(2,1)S(1)} async-done(((bf16[16,4,128,128]{3,2,1,0:T(8,128)(2,1)}), bf16[16,4,128,128]{3,2,1,0:T(8,128)(2,1)S(1)}, u32[]{:S(2)}, u32[]{:S(2)}) %all-to-all-start) | async-done | bytes 2097184 | tf_op jit(solution)/shard_map/all_to_all | solution.py:188
  116.2 0.0 copy-start.5
  116.2 0.9 copy-done.5
  117.1 0.0 copy-start.7
  117.1 0.9 copy-done.7
  118.0 0.0 copy-start.9
  118.0 0.9 copy-done.9
  118.9 0.0 copy-start
  118.9 0.0 copy-start.3
  118.9 0.9 gather_levels.1.mine_ref
  119.8 4.4 %collective-permute-start.5 = (bf16[9,4,128,128]{3,2,1,0:T(8,128)(2,1)S(1)}, bf16[9,4,128,128]{3,2,1,0:T(8,128)(2,1)S(1)}, u32[]{:S(2)}, u32[]{:S(2)}) collective-permute-start(bf16[9,4,128,128]{3,2,1,0:T(8,128)(2,1)S(1)} %gather_levels.1.mine_ref), channel_id=1, source_target_pairs={{0,1},{1,0},{2,3},{3,2},{4,5},{5,4},{6,7},{7,6},{8,9},{9,8},{10,11... | collective-permute-start | bytes 3538952 | tf_op jit(solution)/shard_map/ppermute | solution.py:24
  124.2 2.5 %collective-permute-done.5.their_ref = bf16[9,4,128,128]{3,2,1,0:T(8,128)(2,1)S(1)} collective-permute-done((bf16[9,4,128,128]{3,2,1,0:T(8,128)(2,1)S(1)}, bf16[9,4,128,128]{3,2,1,0:T(8,128)(2,1)S(1)}, u32[]{:S(2)}, u32[]{:S(2)}) %collective-permute-start.5) | collective-permute-done | bytes 1179680 | tf_op jit(solution)/shard_map/ppermute | solution.py:24
  126.6 0.0 copy-done.2
  126.6 0.0 copy-done
  126.6 0.0 copy-done.3
  126.6 7.4 %final_part.1 = bf16[512,1024]{1,0:T(8,128)(2,1)} custom-call(s32[2]{0:T(128)S(1)} %pad_add_fusion.place_ref, bf16[512,1024]{1,0:T(8,128)(2,1)S(1)} %copy-done.2, f32[512,1024]{1,0:T(8,128)S(1)} %copy-done, f32[8,16,512]{2,1,0:T(8,128)S(1)} %copy-done.3, bf16[9,4,128,128]{3,2,1,0:T(8,128)(2,1)S(1)} %gather_levels.1.mine_ref, ...), custom_call_target="tpu_custom_call" | custom-call | tf_op jit(solution)/shard_map/final_part/pallas_call | solution.py:148
  (1 shorter events, 0.0 us)
Async XLA Ops:
  3.7 12.4 %collective-permute-start = (bf16[4,128,128]{2,1,0:T(8,128)(2,1)}, bf16[4,128,128]{2,1,0:T(8,128)(2,1)S(1)}, u32[]{:S(2)}, u32[]{:S(2)}) collective-permute-start(bf16[4,128,128]{2,1,0:T(8,128)(2,1)} %half_state.3), channel_id=1, source_target_pairs={{0,1},{1,0},{2,3},{3,2},{4,5},{5,4},{6,7},{7,6},{8,9},{9,8},{10,11... | collective-permute-start | bytes 393224 | tf_op jit(solution)/shard_map/ppermute | solution.py:24
  16.1 63.5 %copy-start.1 = (bf16[4,128,128]{2,1,0:T(8,128)(2,1)S(1)}, bf16[4,128,128]{2,1,0:T(8,128)(2,1)}, u32[]{:S(2)}) copy-start(bf16[4,128,128]{2,1,0:T(8,128)(2,1)} %half_state.2.other_ref) | copy-start | bytes 393220
  17.1 6.9 %collective-permute-start.1 = (bf16[4,128,128]{2,1,0:T(8,128)(2,1)S(1)}, bf16[4,128,128]{2,1,0:T(8,128)(2,1)S(1)}, u32[]{:S(2)}, u32[]{:S(2)}) collective-permute-start(bf16[4,128,128]{2,1,0:T(8,128)(2,1)S(1)} %fusion.1), channel_id=1, source_target_pairs={{0,2},{1,3},{2,0},{3,1},{4,6},{5,7},{6,4},{7,5},{8,10},{9,11},{10,... | collective-permute-start | bytes 393224 | tf_op jit(solution)/shard_map/ppermute | solution.py:24
  25.0 11.0 %collective-permute-start.2 = (bf16[4,128,128]{2,1,0:T(8,128)(2,1)S(1)}, bf16[4,128,128]{2,1,0:T(8,128)(2,1)S(1)}, u32[]{:S(2)}, u32[]{:S(2)}) collective-permute-start(bf16[4,128,128]{2,1,0:T(8,128)(2,1)S(1)} %fusion.5), channel_id=1, source_target_pairs={{0,4},{1,5},{2,6},{3,7},{4,0},{5,1},{6,2},{7,3},{8,12},{9,13},{10,... | collective-permute-start | bytes 393224 | tf_op jit(solution)/shard_map/ppermute | solution.py:24
  36.0 45.5 %copy-start.4 = (bf16[4,128,128]{2,1,0:T(8,128)(2,1)}, bf16[4,128,128]{2,1,0:T(8,128)(2,1)S(1)}, u32[]{:S(2)}) copy-start(bf16[4,128,128]{2,1,0:T(8,128)(2,1)S(1)} %collective-permute-done.2.refs_1_) | copy-start | bytes 393220
  37.0 17.0 %collective-permute-start.3 = (bf16[4,128,128]{2,1,0:T(8,128)(2,1)S(1)}, bf16[4,128,128]{2,1,0:T(8,128)(2,1)S(1)}, u32[]{:S(2)}, u32[]{:S(2)}) collective-permute-start(bf16[4,128,128]{2,1,0:T(8,128)(2,1)S(1)} %fusion.2), channel_id=1, source_target_pairs={{0,8},{1,9},{2,10},{3,11},{4,12},{5,13},{6,14},{7,15},{8,0},{9,1},... | collective-permute-start | bytes 393224 | tf_op jit(solution)/shard_map/ppermute | solution.py:24
  54.1 27.4 %copy-start.6 = (bf16[4,128,128]{2,1,0:T(8,128)(2,1)}, bf16[4,128,128]{2,1,0:T(8,128)(2,1)S(1)}, u32[]{:S(2)}) copy-start(bf16[4,128,128]{2,1,0:T(8,128)(2,1)S(1)} %collective-permute-done.3.refs_2_) | copy-start | bytes 393220
  55.1 24.4 %collective-permute-start.4 = (bf16[4,128,128]{2,1,0:T(8,128)(2,1)S(1)}, bf16[4,128,128]{2,1,0:T(8,128)(2,1)S(1)}, u32[]{:S(2)}, u32[]{:S(2)}) collective-permute-start(bf16[4,128,128]{2,1,0:T(8,128)(2,1)S(1)} %fusion.3), channel_id=1, source_target_pairs={{0,16},{1,17},{2,18},{3,19},{4,20},{5,21},{6,22},{7,23},{8,24},{9,... | collective-permute-start | bytes 393224 | tf_op jit(solution)/shard_map/ppermute | solution.py:24
  79.5 2.0 %copy-start.8 = (bf16[4,128,128]{2,1,0:T(8,128)(2,1)}, bf16[4,128,128]{2,1,0:T(8,128)(2,1)S(1)}, u32[]{:S(2)}) copy-start(bf16[4,128,128]{2,1,0:T(8,128)(2,1)S(1)} %collective-permute-done.4.refs_3_) | copy-start | bytes 393220
  81.5 5.1 %copy-start.11 = (f32[13]{0:T(128)S(1)}, f32[13]{0:T(128)}, u32[]{:S(2)}) copy-start(f32[13]{0:T(128)} %constant.47.clone) | copy-start | bytes 160
  81.5 5.2 %copy-start.10 = (f32[13,8,512]{2,1,0:T(8,128)S(1)}, f32[13,8,512]{2,1,0:T(8,128)}, u32[]{:S(2)}) copy-start(f32[13,8,512]{2,1,0:T(8,128)} %param.8) | copy-start | bytes 638980
  81.5 34.7 %all-to-all-start = ((bf16[16,4,128,128]{3,2,1,0:T(8,128)(2,1)}), bf16[16,4,128,128]{3,2,1,0:T(8,128)(2,1)S(1)}, u32[]{:S(2)}, u32[]{:S(2)}) async-start(bf16[16,4,128,128]{3,2,1,0:T(8,128)(2,1)} %broadcast_in_dim.16), calls=%async_computation | async-start | bytes 4194304 | tf_op jit(solution)/shard_map/all_to_all | solution.py:188
  97.1 29.5 %copy-start.2 = (bf16[512,1024]{1,0:T(8,128)(2,1)S(1)}, bf16[512,1024]{1,0:T(8,128)(2,1)}, u32[]{:S(2)}) copy-start(bf16[512,1024]{1,0:T(8,128)(2,1)} %q_ref.3) | copy-start | bytes 3145732
  116.2 0.9 copy-start.5
  117.1 0.9 copy-start.7
  118.0 0.9 copy-start.9
  118.9 7.7 %copy-start = (f32[512,1024]{1,0:T(8,128)S(1)}, f32[512,1024]{1,0:T(8,128)}, u32[]{:S(2)}) copy-start(f32[512,1024]{1,0:T(8,128)} %local_part.1.a_ref) | copy-start | bytes 6291460
  118.9 7.7 %copy-start.3 = (f32[8,16,512]{2,1,0:T(8,128)S(1)}, f32[8,16,512]{2,1,0:T(8,128)}, u32[]{:S(2)}) copy-start(f32[8,16,512]{2,1,0:T(8,128)} %pad.4.s_ref) | copy-start | bytes 786436
  119.8 6.8 %collective-permute-start.5 = (bf16[9,4,128,128]{3,2,1,0:T(8,128)(2,1)S(1)}, bf16[9,4,128,128]{3,2,1,0:T(8,128)(2,1)S(1)}, u32[]{:S(2)}, u32[]{:S(2)}) collective-permute-start(bf16[9,4,128,128]{3,2,1,0:T(8,128)(2,1)S(1)} %gather_levels.1.mine_ref), channel_id=1, source_target_pairs={{0,1},{1,0},{2,3},{3,2},{4,5},{5,4},{6,7},{7,6},{8,9},{9,8},{10,11... | collective-permute-start | bytes 3538952 | tf_op jit(solution)/shard_map/ppermute | solution.py:24

commit v2 on v0

v2 whole, which is shorter than its diff:
```python
import functools
import math

import jax
import jax.numpy as jnp
from jax import lax
from jax.experimental import pallas as pl
from jax.experimental.pallas import tpu as pltpu
from jax.sharding import PartitionSpec as P

DK = 128
STRETCH = 64
F32 = jnp.float32
BF16 = jnp.bfloat16


def level_factor(level_num):
    token_count = STRETCH if level_num == 0 else STRETCH * 2 ** (level_num - 1)
    return 1.0 / math.sqrt(DK * token_count)


def swap(block, axis, stride):
    count = lax.axis_size(axis)
    return lax.ppermute(block, axis, [(i, i ^ stride) for i in range(count)])


def on_chip(x):
    return pltpu.with_memory_space_constraint(x, pltpu.VMEM)


def vmem_call(kernel, out_shapes, scalars, operands, name, limit_mib=32, flops=0):
    many = isinstance(out_shapes, (list, tuple))
    vmem = pl.BlockSpec(memory_space=pltpu.VMEM)
    moved = sum(x.size * x.dtype.itemsize for x in operands)
    return pl.pallas_call(
        kernel,
        out_shape=out_shapes,
        in_specs=[pl.BlockSpec(memory_space=pltpu.SMEM)] + [vmem] * len(operands),
        out_specs=[vmem] * len(out_shapes) if many else vmem,
        compiler_params=pltpu.CompilerParams(vmem_limit_bytes=limit_mib << 20),
        cost_estimate=pl.CostEstimate(flops=flops, transcendentals=0, bytes_accessed=moved),
        name=name,
    )(scalars, *operands)


def lanes(head):
    start = head * DK
    return pl.ds(start if isinstance(start, int) else pl.multiple_of(start, DK), DK)


def state_kernel(place_ref, k_ref, v_ref, send_ref, keep_ref):
    half = send_ref.shape[0]
    for o_ref, side in ((send_ref, 1 - place_ref[1]), (keep_ref, place_ref[1])):
        for n in range(half):
            at = lanes(side * half + n)
            o_ref[n] = lax.dot_general(
                v_ref[:, at], k_ref[:, at], (((0,), (0,)), ((), ())), preferred_element_type=F32
            ).astype(BF16)


def local_kernel(place_ref, q_ref, k_ref, v_ref, s_ref, o_ref):
    rows = q_ref.shape[0]
    tile = 2 * STRETCH
    key = lax.broadcasted_iota(jnp.int32, (tile, tile), 0)
    tok = lax.broadcasted_iota(jnp.int32, (tile, tile), 1)
    low = jnp.logical_and(tok >= STRETCH, key < STRETCH)
    same = jnp.logical_and(key <= tok, jnp.logical_not(low))
    for head in range(o_ref.shape[0]):
        at = lanes(head)
        value_t = v_ref[:, at].T
        for r in range(rows // tile):
            here = pl.ds(r * tile, tile)
            span = (r + 1) * tile
            score = lax.dot_general(
                k_ref[pl.ds(0, span), at], q_ref[here, at], (((1,), (1,)), ((), ())),
                preferred_element_type=F32,
            )
            parts = []
            for c in range(r):
                level = 1 + (r ^ c).bit_length()
                parts.append(score[c * tile : (c + 1) * tile] * s_ref[head, pl.ds(level, 1), here])
            weight = jnp.where(
                same, s_ref[head, pl.ds(0, 1), here], jnp.where(low, s_ref[head, pl.ds(1, 1), here], 0.0)
            )
            parts.append(score[r * tile :] * weight)
            weighted = jnp.concatenate([p.astype(BF16) for p in parts], axis=0)
            o_ref[head, :, here] = jnp.dot(value_t[:, :span], weighted, preferred_element_type=F32)


def sums_kernel(bits, place_ref, *refs):
    had, (all_ref, o_ref) = refs[:-2], refs[-2:]
    own = place_ref[0]
    for b, ref in enumerate(had):
        o_ref[b] = ref[0]
    for b in range(bits):
        low = jnp.maximum(lax.shift_right_logical(own, b) - 1, 0) * 2**b
        total = all_ref[low].astype(F32)
        for i in range(1, 2**b):
            total = total + all_ref[low + i].astype(F32)
        o_ref[len(had) + b] = total.astype(BF16)


def final_kernel(early, first_level, place_ref, q_ref, a_ref, s_ref, mine_ref, their_ref, o_ref):
    half = a_ref.shape[0] // 2
    late = mine_ref.shape[0] // half - early
    for states, side in ((mine_ref, place_ref[1]), (their_ref, 1 - place_ref[1])):
        for slot in range(half):
            n = place_ref[2] ^ (slot // 2 | slot % 2 * 2)
            head = side * half + n
            at = lanes(head)
            query = q_ref[:, at]
            total = a_ref[head]
            found = [states[level * half + n] for level in range(early)]
            found.append(states[pl.ds(early * half + slot * late, late)].reshape(late * DK, DK))
            part = lax.dot_general(
                jnp.concatenate(found, axis=0), query, (((1,), (1,)), ((), ())), preferred_element_type=F32
            )
            for j in range(early + late):
                total = total + part[j * DK : (j + 1) * DK] * s_ref[head, pl.ds(first_level + j, 1), :]
            o_ref[:, at] = total.T.astype(BF16)


def on_device(queries, keys, values, level_weights):
    rows, width = queries.shape
    heads = width // DK
    half = heads // 2
    local_bits = (rows // STRETCH).bit_length() - 1
    ctx_bits = lax.axis_size("ctx").bit_length() - 1
    runs = lax.axis_size("grp")
    grp_bits = runs.bit_length() - 1
    ctx_index = lax.axis_index("ctx").astype(jnp.int32)
    grp_index = lax.axis_index("grp").astype(jnp.int32)
    core = ctx_index & 1
    quarter = lax.shift_right_logical(ctx_index, 1) & 3
    place = jnp.stack([grp_index, core, quarter])

    block = grp_index * lax.axis_size("ctx") + ctx_index
    level_ids = jnp.arange(level_weights.shape[0], dtype=jnp.int32)
    bit_of = jnp.maximum(level_ids - 1 - local_bits, 0)
    live = jnp.logical_or(level_ids <= local_bits, jnp.right_shift(block, bit_of) % 2 == 1)
    factor = jnp.asarray([level_factor(n) for n in range(level_weights.shape[0])], F32)
    gain = jnp.where(live, factor, 0.0)
    scales = jnp.transpose(level_weights * gain[:, None, None], (1, 0, 2))
    scales = jnp.pad(scales, ((0, 0), (0, -scales.shape[1] % 8), (0, 0)))

    state = jax.ShapeDtypeStruct((half, DK, DK), BF16)
    send, keep = vmem_call(
        state_kernel, [state, state], place, [keys, values], "block_states", 16, 2 * rows * DK * width
    )
    first = swap(send, "ctx", 1)
    running = keep.astype(F32) + first.astype(F32)
    early = [jnp.where(core == 1, first, keep)]
    for b in (1, 2):
        early.append(swap(running.astype(BF16), "ctx", 1 << b))
        running = running + early[-1].astype(F32)

    running = lax.dynamic_slice_in_dim(running, quarter, 1, 0)
    late = []
    for b in range(3, ctx_bits):
        late.append(swap(running.astype(BF16), "ctx", 1 << b))
        running = running + late[-1].astype(F32)
    group_states = lax.all_to_all(
        jnp.broadcast_to(running.astype(BF16), (runs, DK, DK)), "grp", 0, 0, tiled=True
    )
    local = vmem_call(
        local_kernel,
        jax.ShapeDtypeStruct((heads, DK, rows), F32),
        place,
        [queries, keys, values, scales],
        "local_part",
        32,
        4 * rows * rows * width,
    )
    group_states, local = lax.optimization_barrier((group_states, local))
    levels = len(late) + grp_bits
    one = vmem_call(
        functools.partial(sums_kernel, grp_bits),
        jax.ShapeDtypeStruct((levels, DK, DK), BF16),
        place,
        [*late, on_chip(group_states)],
        "run_sums",
        16,
    )
    two = jnp.concatenate([one, swap(one, "ctx", 4)], axis=0)
    four = [two, swap(two, "ctx", 2)]
    mine = jnp.concatenate(early + four, axis=0)
    theirs = swap(mine, "ctx", 1)
    return vmem_call(
        functools.partial(final_kernel, len(early), 1 + local_bits),
        jax.ShapeDtypeStruct((rows, width), BF16),
        place,
        [queries, local, scales, on_chip(mine), on_chip(theirs)],
        "final_part",
        32,
        2 * rows * DK * width * (3 + levels),
    )


def solution(mesh):
    return jax.shard_map(
        on_device,
        mesh=mesh,
        in_specs=(
            P(("grp", "ctx"), None),
            P(("grp", "ctx"), None),
            P(("grp", "ctx"), None),
            P(None, None, ("grp", "ctx")),
        ),
        out_specs=P(("grp", "ctx"), None),
        check_vma=False,
    )
```

time: 257 us -> 107 us (0.42)
  waiting for transfers between devices: 177 us -> 46.6 us
  matrix products: 25.2 us -> 0 us
  between operations: 13.7 us -> 0.28 us
  starting transfers between devices: 27 us -> 38.8 us
  Pallas kernels: 0 us -> 10.6 us
  other arithmetic: 4.59 us -> 1.36 us
    ppermute x5 -> x8, waiting for transfers between devices: 117 us -> 43.4 us  [swap(): return lax.ppermute(block, axis, [(i, i ^ stride) for i in range(count)])]
    all_gather x1 -> x0, waiting for transfers between devices: 60 us -> none  [on_device(): lax.all_gather(group_state[None], 'grp', axis=0, tiled=True)]
    dot_general x12 -> x0, matrix products: 25.2 us -> none  [the longest x9 12.3 us: on_device(): jnp.einsum('ryl,ylf->ryf', query_matrix, siblings[bit_num].astype(jnp.bfl...]
    pallas_call x0 -> x4, Pallas kernels: none -> 10.6 us  [vmem_call(): pl.pallas_call(kernel, out_shape=out_shapes, in_specs=[pl.BlockSpec(memor...]
    ppermute x5 -> x8, starting transfers between devices: 27 us -> 34.6 us  [swap(): return lax.ppermute(block, axis, [(i, i ^ stride) for i in range(count)])]
    all_to_all x0 -> x1, starting transfers between devices: none -> 4.24 us  [on_device(): lax.all_to_all(jnp.broadcast_to(running.astype(BF16), (runs, DK, DK)), 'g...]
    unnamed x40 -> x38, local copies, waits for them, and re-layouts: 3.06 us -> 7.13 us
    all_to_all x0 -> x1, waiting for transfers between devices: none -> 3.27 us  [on_device(): lax.all_to_all(jnp.broadcast_to(running.astype(BF16), (runs, DK, DK)), 'g...]
  transfers between devices with their start and end apart: 6 -> 9, of which waited for: 6 -> 9; matrix products, arithmetic and copies ran while one was open for 7% -> 1% of each run, Pallas kernels for 0% -> 4%
where the time goes in v2:
time: 107 us; the launch traced here: 106 us
  waiting for transfers between devices  46.6 us (44%)
  starting transfers between devices  38.8 us (36%)
  Pallas kernels  10.6 us (10%)
  local copies, waits for them, and re-layouts  8.1 us (8%)
  other arithmetic  1.36 us (1%)
    ppermute x8, waiting for transfers between devices, swap(): return lax.ppermute(block, axis, [(i, i ^ stride) for i in range(count)])  43.4 us
    ppermute x8, starting transfers between devices, swap(): return lax.ppermute(block, axis, [(i, i ^ stride) for i in range(count)])  34.6 us
    pallas_call x4, Pallas kernels, vmem_call(): pl.pallas_call(kernel, out_shape=out_shapes, in_specs=[pl.BlockSpec(memor...  10.6 us
    unnamed x38, local copies, waits for them, and re-layouts  7.13 us
    all_to_all x1, starting transfers between devices, on_device(): lax.all_to_all(jnp.broadcast_to(running.astype(BF16), (runs, DK, DK)), 'g...  4.24 us
    all_to_all x1, waiting for transfers between devices, on_device(): lax.all_to_all(jnp.broadcast_to(running.astype(BF16), (runs, DK, DK)), 'g...  3.27 us
  transfers between devices with their start and end apart: 9, of which 9 were waited for; matrix products, arithmetic and copies ran while one was open for 1% of the time, Pallas kernels for 4%

profile of v2, /device:TPU:1, one launch (start us, length us, event | category | flops | bytes accessed | tf_op | source)
XLA Modules:
  0.0 105.8 jit_solution(5166859021729186554)
XLA Ops:
  0.0 0.1 pad_add_fusion.place_ref
  0.1 0.0 copy-start
  0.1 1.2 %copy-done = bf16[512,1024]{1,0:T(8,128)(2,1)S(1)} copy-done((bf16[512,1024]{1,0:T(8,128)(2,1)S(1)}, bf16[512,1024]{1,0:T(8,128)(2,1)}, u32[]{:S(2)}) %copy-start) | copy-done | bytes 1048600
  1.3 0.0 copy-start.2
  1.3 1.2 %copy-done.2 = bf16[512,1024]{1,0:T(8,128)(2,1)S(1)} copy-done((bf16[512,1024]{1,0:T(8,128)(2,1)S(1)}, bf16[512,1024]{1,0:T(8,128)(2,1)}, u32[]{:S(2)}) %copy-start.2) | copy-done | bytes 1048600
  2.5 1.4 %block_states.1 = (bf16[4,128,128]{2,1,0:T(8,128)(2,1)S(1)}, bf16[4,128,128]{2,1,0:T(8,128)(2,1)S(1)}) custom-call(s32[3]{0:T(128)S(1)} %pad_add_fusion.place_ref, bf16[512,1024]{1,0:T(8,128)(2,1)S(1)} %copy-done, bf16[512,1024]{1,0:T(8,128)(2,1)S(1)} %copy-done.2), custom_call_target="tpu_custom_call" | custom-call | flops 134217728 | bytes 2097152 | tf_op jit(solution)/shard_map/block_states/pallas_call | solution.py:35
  3.9 8.7 %collective-permute-start = (bf16[4,128,128]{2,1,0:T(8,128)(2,1)S(1)}, bf16[4,128,128]{2,1,0:T(8,128)(2,1)S(1)}, u32[]{:S(2)}, u32[]{:S(2)}) collective-permute-start(bf16[4,128,128]{2,1,0:T(8,128)(2,1)S(1)} %get-tuple-element.10), channel_id=1, source_target_pairs={{0,1},{1,0},{2,3},{3,2},{4,5},{5,4},{6,7},{7,6},{8,9},{9,8},{10,11... | collective-permute-start | bytes 393224 | tf_op jit(solution)/shard_map/ppermute | solution.py:24
  12.7 1.0 collective-permute-done
  13.6 0.0 copy-start.10
  13.7 1.9 %collective-permute-start.1 = (bf16[4,128,128]{2,1,0:T(8,128)(2,1)S(1)}, bf16[4,128,128]{2,1,0:T(8,128)(2,1)S(1)}, u32[]{:S(2)}, u32[]{:S(2)}) collective-permute-start(bf16[4,128,128]{2,1,0:T(8,128)(2,1)S(1)} %fusion.1), channel_id=1, source_target_pairs={{0,2},{1,3},{2,0},{3,1},{4,6},{5,7},{6,4},{7,5},{8,10},{9,11},{10,... | collective-permute-start | bytes 393224 | tf_op jit(solution)/shard_map/ppermute | solution.py:24
  15.6 4.7 %collective-permute-done.1 = bf16[4,128,128]{2,1,0:T(8,128)(2,1)S(1)} collective-permute-done((bf16[4,128,128]{2,1,0:T(8,128)(2,1)S(1)}, bf16[4,128,128]{2,1,0:T(8,128)(2,1)S(1)}, u32[]{:S(2)}, u32[]{:S(2)}) %collective-permute-start.1) | collective-permute-done | bytes 131104 | tf_op jit(solution)/shard_map/ppermute | solution.py:24
  20.3 0.0 copy-done.10
  20.3 0.0 copy-start.11
  20.3 0.1 fusion.6
  20.3 0.6 copy-done.11
  20.9 0.0 copy-start.16
  20.9 0.0 copy-start.15
  20.9 2.0 %collective-permute-start.2 = (bf16[4,128,128]{2,1,0:T(8,128)(2,1)S(1)}, bf16[4,128,128]{2,1,0:T(8,128)(2,1)S(1)}, u32[]{:S(2)}, u32[]{:S(2)}) collective-permute-start(bf16[4,128,128]{2,1,0:T(8,128)(2,1)S(1)} %get-tuple-element.13), channel_id=1, source_target_pairs={{0,4},{1,5},{2,6},{3,7},{4,0},{5,1},{6,2},{7,3},{8,12},{9,13},{10,... | collective-permute-start | bytes 393224 | tf_op jit(solution)/shard_map/ppermute | solution.py:24
  23.0 9.1 %collective-permute-done.2 = bf16[4,128,128]{2,1,0:T(8,128)(2,1)S(1)} collective-permute-done((bf16[4,128,128]{2,1,0:T(8,128)(2,1)S(1)}, bf16[4,128,128]{2,1,0:T(8,128)(2,1)S(1)}, u32[]{:S(2)}, u32[]{:S(2)}) %collective-permute-start.2) | collective-permute-done | bytes 131104 | tf_op jit(solution)/shard_map/ppermute | solution.py:24
  32.0 0.0 copy-start.13
  32.1 3.5 %collective-permute-start.3 = (bf16[1,128,128]{2,1,0:T(8,128)(2,1)S(1)}, bf16[1,128,128]{2,1,0:T(8,128)(2,1)S(1)}, u32[]{:S(2)}, u32[]{:S(2)}) collective-permute-start(bf16[1,128,128]{2,1,0:T(8,128)(2,1)S(1)} %fusion.4), channel_id=1, source_target_pairs={{0,8},{1,9},{2,10},{3,11},{4,12},{5,13},{6,14},{7,15},{8,0},{9,1},... | collective-permute-start | bytes 98312 | tf_op jit(solution)/shard_map/ppermute | solution.py:24
  35.6 6.5 %collective-permute-done.3.refs_0_ = bf16[1,128,128]{2,1,0:T(8,128)(2,1)S(1)} collective-permute-done((bf16[1,128,128]{2,1,0:T(8,128)(2,1)S(1)}, bf16[1,128,128]{2,1,0:T(8,128)(2,1)S(1)}, u32[]{:S(2)}, u32[]{:S(2)}) %collective-permute-start.3) | collective-permute-done | bytes 32800 | tf_op jit(solution)/shard_map/ppermute | solution.py:24
  42.1 0.0 copy-start.6
  42.1 8.9 %collective-permute-start.4 = (bf16[1,128,128]{2,1,0:T(8,128)(2,1)S(1)}, bf16[1,128,128]{2,1,0:T(8,128)(2,1)S(1)}, u32[]{:S(2)}, u32[]{:S(2)}) collective-permute-start(bf16[1,128,128]{2,1,0:T(8,128)(2,1)S(1)} %fusion.2), channel_id=1, source_target_pairs={{0,16},{1,17},{2,18},{3,19},{4,20},{5,21},{6,22},{7,23},{8,24},{9,... | collective-permute-start | bytes 98312 | tf_op jit(solution)/shard_map/ppermute | solution.py:24
  51.0 4.8 %collective-permute-done.4.refs_1_ = bf16[1,128,128]{2,1,0:T(8,128)(2,1)S(1)} collective-permute-done((bf16[1,128,128]{2,1,0:T(8,128)(2,1)S(1)}, bf16[1,128,128]{2,1,0:T(8,128)(2,1)S(1)}, u32[]{:S(2)}, u32[]{:S(2)}) %collective-permute-start.4) | collective-permute-done | bytes 32800 | tf_op jit(solution)/shard_map/ppermute | solution.py:24
  55.8 0.0 copy-start.8
  55.8 0.0 copy-start.1
  55.8 0.9 broadcast_in_dim.13
  56.7 4.2 %all-to-all-start = ((bf16[16,128,128]{2,1,0:T(8,128)(2,1)}), bf16[16,128,128]{2,1,0:T(8,128)(2,1)}, u32[]{:S(2)}, u32[]{:S(2)}) async-start(bf16[16,128,128]{2,1,0:T(8,128)(2,1)} %broadcast_in_dim.13), calls=%async_computation | async-start | bytes 1048576 | tf_op jit(solution)/shard_map/all_to_all | solution.py:162
  61.0 0.0 copy-done.13
  61.0 0.0 copy-done.16
  61.0 0.0 copy-done.15
  61.0 0.1 fusion
  61.2 0.0 copy-done.6
  61.2 0.0 copy-done.8
  61.2 0.0 copy-done.1
  61.2 0.0 copy-start.3
  61.2 1.2 %copy-done.3 = bf16[512,1024]{1,0:T(8,128)(2,1)S(1)} copy-done((bf16[512,1024]{1,0:T(8,128)(2,1)S(1)}, bf16[512,1024]{1,0:T(8,128)(2,1)}, u32[]{:S(2)}) %copy-start.3) | copy-done | bytes 1048600
  62.5 0.0 copy-start.4
  62.5 1.2 %copy-done.4 = bf16[512,1024]{1,0:T(8,128)(2,1)S(1)} copy-done((bf16[512,1024]{1,0:T(8,128)(2,1)S(1)}, bf16[512,1024]{1,0:T(8,128)(2,1)}, u32[]{:S(2)}) %copy-start.4) | copy-done | bytes 1048600
  63.7 3.8 %local_part.1.a_ref = f32[8,128,512]{2,1,0:T(8,128)S(1)} custom-call(s32[3]{0:T(128)S(1)} %pad_add_fusion.place_ref, bf16[512,1024]{1,0:T(8,128)(2,1)S(1)} %copy-done.4, bf16[512,1024]{1,0:T(8,128)(2,1)S(1)} %copy-done.1, bf16[512,1024]{1,0:T(8,128)(2,1)S(1)} %copy-done.3, f32[8,16,512]{2,1,0:T(8,128)S(1)} %pad.4.s_ref), custom_call_target="tpu_custom_call" | custom-call | flops 1073741824 | bytes 3407872 | tf_op jit(solution)/shard_map/local_part/pallas_call | solution.py:35
  67.5 3.3 %all-to-all-done.refs_2_ = bf16[16,128,128]{2,1,0:T(8,128)(2,1)} async-done(((bf16[16,128,128]{2,1,0:T(8,128)(2,1)}), bf16[16,128,128]{2,1,0:T(8,128)(2,1)}, u32[]{:S(2)}, u32[]{:S(2)}) %all-to-all-start) | async-done | bytes 524320 | tf_op jit(solution)/shard_map/all_to_all | solution.py:162
  70.8 0.0 copy-start.7
  70.8 0.8 copy-done.7
  71.5 0.0 copy-start.9
  71.5 0.8 copy-done.9
  72.3 0.0 copy-start.12
  72.3 0.0 copy-start.14
  72.3 1.2 %run_sums.1 = bf16[6,128,128]{2,1,0:T(8,128)(2,1)S(1)} custom-call(s32[3]{0:T(128)S(1)} %pad_add_fusion.place_ref, bf16[1,128,128]{2,1,0:T(8,128)(2,1)S(1)} %copy-done.7, bf16[1,128,128]{2,1,0:T(8,128)(2,1)S(1)} %copy-done.9, bf16[16,128,128]{2,1,0:T(8,128)(2,1)} %all-to-all-done.refs_2_), custom_call_target="tpu_custom_call" | custom-call | bytes 589824 | tf_op jit(solution)/shard_map/run_sums/pallas_call | solution.py:35
  73.5 1.9 %collective-permute-start.5 = (bf16[6,128,128]{2,1,0:T(8,128)(2,1)S(1)}, bf16[6,128,128]{2,1,0:T(8,128)(2,1)S(1)}, u32[]{:S(2)}, u32[]{:S(2)}) collective-permute-start(bf16[6,128,128]{2,1,0:T(8,128)(2,1)S(1)} %run_sums.1), channel_id=1, source_target_pairs={{0,4},{1,5},{2,6},{3,7},{4,0},{5,1},{6,2},{7,3},{8,12},{9,13},{10,... | collective-permute-start | bytes 589832 | tf_op jit(solution)/shard_map/ppermute | solution.py:24
  75.4 1.0 select_dynamic-update-slice_fusion
  76.3 7.2 %collective-permute-done.5 = bf16[6,128,128]{2,1,0:T(8,128)(2,1)S(1)} collective-permute-done((bf16[6,128,128]{2,1,0:T(8,128)(2,1)S(1)}, bf16[6,128,128]{2,1,0:T(8,128)(2,1)S(1)}, u32[]{:S(2)}, u32[]{:S(2)}) %collective-permute-start.5) | collective-permute-done | bytes 196640 | tf_op jit(solution)/shard_map/ppermute | solution.py:24
  83.6 0.0 copy-start.5
  83.6 2.4 %collective-permute-start.6 = (bf16[12,128,128]{2,1,0:T(8,128)(2,1)S(1)}, bf16[12,128,128]{2,1,0:T(8,128)(2,1)S(1)}, u32[]{:S(2)}, u32[]{:S(2)}) collective-permute-start(bf16[12,128,128]{2,1,0:T(8,128)(2,1)S(1)} %pad_maximum_fusion), channel_id=1, source_target_pairs={{0,2},{1,3},{2,0},{3,1},{4,6},{5,7},{6,4},{7,5},{8,10},{9,11},{10,... | collective-permute-start | bytes 1179656 | tf_op jit(solution)/shard_map/ppermute | solution.py:24
  86.0 0.0 copy-done.12
  86.0 0.0 copy-done.14
  86.1 7.7 %collective-permute-done.6 = bf16[12,128,128]{2,1,0:T(8,128)(2,1)S(1)} collective-permute-done((bf16[12,128,128]{2,1,0:T(8,128)(2,1)S(1)}, bf16[12,128,128]{2,1,0:T(8,128)(2,1)S(1)}, u32[]{:S(2)}, u32[]{:S(2)}) %collective-permute-start.6) | collective-permute-done | bytes 393248 | tf_op jit(solution)/shard_map/ppermute | solution.py:24
  93.8 0.1 constant_dynamic-update-slice_fusion.mine_ref
  93.9 5.2 %collective-permute-start.7 = (bf16[36,128,128]{2,1,0:T(8,128)(2,1)S(1)}, bf16[36,128,128]{2,1,0:T(8,128)(2,1)S(1)}, u32[]{:S(2)}, u32[]{:S(2)}) collective-permute-start(bf16[36,128,128]{2,1,0:T(8,128)(2,1)S(1)} %constant_dynamic-update-slice_fusion.mine_ref), channel_id=1, source_target_pairs={{0,1},{1,0},{2,3},{3,2},{4,5},{5,4},{6,7},{7,6},{8,9},{9,8},{10,11... | collective-permute-start | bytes 3538952 | tf_op jit(solution)/shard_map/ppermute | solution.py:24
  99.1 2.5 %collective-permute-done.7.their_ref = bf16[36,128,128]{2,1,0:T(8,128)(2,1)S(1)} collective-permute-done((bf16[36,128,128]{2,1,0:T(8,128)(2,1)S(1)}, bf16[36,128,128]{2,1,0:T(8,128)(2,1)S(1)}, u32[]{:S(2)}, u32[]{:S(2)}) %collective-permute-start.7) | collective-permute-done | bytes 1179680 | tf_op jit(solution)/shard_map/ppermute | solution.py:24
  101.6 0.0 copy-done.5
  101.6 4.3 %final_part.1 = bf16[512,1024]{1,0:T(8,128)(2,1)} custom-call(s32[3]{0:T(128)S(1)} %pad_add_fusion.place_ref, bf16[512,1024]{1,0:T(8,128)(2,1)S(1)} %copy-done.5, f32[8,128,512]{2,1,0:T(8,128)S(1)} %local_part.1.a_ref, f32[8,16,512]{2,1,0:T(8,128)S(1)} %pad.4.s_ref, bf16[36,128,128]{2,1,0:T(8,128)(2,1)S(1)} %constant_dynamic-update-slice_fusion.mine_ref, ...), custom_call_target="tpu_custom_call" | custom-call | flops 1207959552 | bytes 5767168 | tf_op jit(solution)/shard_map/final_part/pallas_call | solution.py:35
  (11 shorter events, 0.3 us)
Async XLA Ops:
  0.1 1.2 %copy-start = (bf16[512,1024]{1,0:T(8,128)(2,1)S(1)}, bf16[512,1024]{1,0:T(8,128)(2,1)}, u32[]{:S(2)}) copy-start(bf16[512,1024]{1,0:T(8,128)(2,1)} %k_ref.3) | copy-start | bytes 3145732
  1.3 1.2 %copy-start.2 = (bf16[512,1024]{1,0:T(8,128)(2,1)S(1)}, bf16[512,1024]{1,0:T(8,128)(2,1)}, u32[]{:S(2)}) copy-start(bf16[512,1024]{1,0:T(8,128)(2,1)} %v_ref.3) | copy-start | bytes 3145732
  3.9 9.7 %collective-permute-start = (bf16[4,128,128]{2,1,0:T(8,128)(2,1)S(1)}, bf16[4,128,128]{2,1,0:T(8,128)(2,1)S(1)}, u32[]{:S(2)}, u32[]{:S(2)}) collective-permute-start(bf16[4,128,128]{2,1,0:T(8,128)(2,1)S(1)} %get-tuple-element.10), channel_id=1, source_target_pairs={{0,1},{1,0},{2,3},{3,2},{4,5},{5,4},{6,7},{7,6},{8,9},{9,8},{10,11... | collective-permute-start | bytes 393224 | tf_op jit(solution)/shard_map/ppermute | solution.py:24
  13.6 6.6 %copy-start.10 = (bf16[4,128,128]{2,1,0:T(8,128)(2,1)}, bf16[4,128,128]{2,1,0:T(8,128)(2,1)S(1)}, u32[]{:S(2)}) copy-start(bf16[4,128,128]{2,1,0:T(8,128)(2,1)S(1)} %collective-permute-done) | copy-start | bytes 393220
  13.7 6.6 %collective-permute-start.1 = (bf16[4,128,128]{2,1,0:T(8,128)(2,1)S(1)}, bf16[4,128,128]{2,1,0:T(8,128)(2,1)S(1)}, u32[]{:S(2)}, u32[]{:S(2)}) collective-permute-start(bf16[4,128,128]{2,1,0:T(8,128)(2,1)S(1)} %fusion.1), channel_id=1, source_target_pairs={{0,2},{1,3},{2,0},{3,1},{4,6},{5,7},{6,4},{7,5},{8,10},{9,11},{10,... | collective-permute-start | bytes 393224 | tf_op jit(solution)/shard_map/ppermute | solution.py:24
  20.3 0.6 copy-start.11
  20.9 40.1 %copy-start.16 = (f32[13]{0:T(128)S(1)}, f32[13]{0:T(128)}, u32[]{:S(2)}) copy-start(f32[13]{0:T(128)} %constant.44.clone) | copy-start | bytes 160
  20.9 40.1 %copy-start.15 = (f32[13,8,512]{2,1,0:T(8,128)S(1)}, f32[13,8,512]{2,1,0:T(8,128)}, u32[]{:S(2)}) copy-start(f32[13,8,512]{2,1,0:T(8,128)} %param.8) | copy-start | bytes 638980
  20.9 11.1 %collective-permute-start.2 = (bf16[4,128,128]{2,1,0:T(8,128)(2,1)S(1)}, bf16[4,128,128]{2,1,0:T(8,128)(2,1)S(1)}, u32[]{:S(2)}, u32[]{:S(2)}) collective-permute-start(bf16[4,128,128]{2,1,0:T(8,128)(2,1)S(1)} %get-tuple-element.13), channel_id=1, source_target_pairs={{0,4},{1,5},{2,6},{3,7},{4,0},{5,1},{6,2},{7,3},{8,12},{9,13},{10,... | collective-permute-start | bytes 393224 | tf_op jit(solution)/shard_map/ppermute | solution.py:24
  32.0 28.9 %copy-start.13 = (bf16[4,128,128]{2,1,0:T(8,128)(2,1)}, bf16[4,128,128]{2,1,0:T(8,128)(2,1)S(1)}, u32[]{:S(2)}) copy-start(bf16[4,128,128]{2,1,0:T(8,128)(2,1)S(1)} %collective-permute-done.2) | copy-start | bytes 393220
  32.1 10.0 %collective-permute-start.3 = (bf16[1,128,128]{2,1,0:T(8,128)(2,1)S(1)}, bf16[1,128,128]{2,1,0:T(8,128)(2,1)S(1)}, u32[]{:S(2)}, u32[]{:S(2)}) collective-permute-start(bf16[1,128,128]{2,1,0:T(8,128)(2,1)S(1)} %fusion.4), channel_id=1, source_target_pairs={{0,8},{1,9},{2,10},{3,11},{4,12},{5,13},{6,14},{7,15},{8,0},{9,1},... | collective-permute-start | bytes 98312 | tf_op jit(solution)/shard_map/ppermute | solution.py:24
  42.1 19.1 %copy-start.6 = (bf16[1,128,128]{2,1,0:T(8,128)(2,1)}, bf16[1,128,128]{2,1,0:T(8,128)(2,1)S(1)}, u32[]{:S(2)}) copy-start(bf16[1,128,128]{2,1,0:T(8,128)(2,1)S(1)} %collective-permute-done.3.refs_0_) | copy-start | bytes 98308
  42.1 13.7 %collective-permute-start.4 = (bf16[1,128,128]{2,1,0:T(8,128)(2,1)S(1)}, bf16[1,128,128]{2,1,0:T(8,128)(2,1)S(1)}, u32[]{:S(2)}, u32[]{:S(2)}) collective-permute-start(bf16[1,128,128]{2,1,0:T(8,128)(2,1)S(1)} %fusion.2), channel_id=1, source_target_pairs={{0,16},{1,17},{2,18},{3,19},{4,20},{5,21},{6,22},{7,23},{8,24},{9,... | collective-permute-start | bytes 98312 | tf_op jit(solution)/shard_map/ppermute | solution.py:24
  55.8 5.4 %copy-start.8 = (bf16[1,128,128]{2,1,0:T(8,128)(2,1)}, bf16[1,128,128]{2,1,0:T(8,128)(2,1)S(1)}, u32[]{:S(2)}) copy-start(bf16[1,128,128]{2,1,0:T(8,128)(2,1)S(1)} %collective-permute-done.4.refs_1_) | copy-start | bytes 98308
  55.8 5.4 %copy-start.1 = (bf16[512,1024]{1,0:T(8,128)(2,1)S(1)}, bf16[512,1024]{1,0:T(8,128)(2,1)}, u32[]{:S(2)}) copy-start(bf16[512,1024]{1,0:T(8,128)(2,1)} %k_ref.3) | copy-start | bytes 3145732
  56.7 14.0 %all-to-all-start = ((bf16[16,128,128]{2,1,0:T(8,128)(2,1)}), bf16[16,128,128]{2,1,0:T(8,128)(2,1)}, u32[]{:S(2)}, u32[]{:S(2)}) async-start(bf16[16,128,128]{2,1,0:T(8,128)(2,1)} %broadcast_in_dim.13), calls=%async_computation | async-start | bytes 1048576 | tf_op jit(solution)/shard_map/all_to_all | solution.py:162
  61.2 1.2 %copy-start.3 = (bf16[512,1024]{1,0:T(8,128)(2,1)S(1)}, bf16[512,1024]{1,0:T(8,128)(2,1)}, u32[]{:S(2)}) copy-start(bf16[512,1024]{1,0:T(8,128)(2,1)} %v_ref.3) | copy-start | bytes 3145732
  62.5 1.2 %copy-start.4 = (bf16[512,1024]{1,0:T(8,128)(2,1)S(1)}, bf16[512,1024]{1,0:T(8,128)(2,1)}, u32[]{:S(2)}) copy-start(bf16[512,1024]{1,0:T(8,128)(2,1)} %q_ref.3) | copy-start | bytes 3145732
  70.8 0.8 copy-start.7
  71.5 0.8 copy-start.9
  72.3 13.7 %copy-start.12 = (bf16[4,128,128]{2,1,0:T(8,128)(2,1)S(1)}, bf16[4,128,128]{2,1,0:T(8,128)(2,1)}, u32[]{:S(2)}) copy-start(bf16[4,128,128]{2,1,0:T(8,128)(2,1)} %copy-done.11) | copy-start | bytes 393220
  72.3 13.7 %copy-start.14 = (bf16[4,128,128]{2,1,0:T(8,128)(2,1)S(1)}, bf16[4,128,128]{2,1,0:T(8,128)(2,1)}, u32[]{:S(2)}) copy-start(bf16[4,128,128]{2,1,0:T(8,128)(2,1)} %copy-done.13) | copy-start | bytes 393220
  73.5 10.1 %collective-permute-start.5 = (bf16[6,128,128]{2,1,0:T(8,128)(2,1)S(1)}, bf16[6,128,128]{2,1,0:T(8,128)(2,1)S(1)}, u32[]{:S(2)}, u32[]{:S(2)}) collective-permute-start(bf16[6,128,128]{2,1,0:T(8,128)(2,1)S(1)} %run_sums.1), channel_id=1, source_target_pairs={{0,4},{1,5},{2,6},{3,7},{4,0},{5,1},{6,2},{7,3},{8,12},{9,13},{10,... | collective-permute-start | bytes 589832 | tf_op jit(solution)/shard_map/ppermute | solution.py:24
  83.6 18.0 %copy-start.5 = (bf16[512,1024]{1,0:T(8,128)(2,1)S(1)}, bf16[512,1024]{1,0:T(8,128)(2,1)}, u32[]{:S(2)}) copy-start(bf16[512,1024]{1,0:T(8,128)(2,1)} %q_ref.3) | copy-start | bytes 3145732
  83.6 10.2 %collective-permute-start.6 = (bf16[12,128,128]{2,1,0:T(8,128)(2,1)S(1)}, bf16[12,128,128]{2,1,0:T(8,128)(2,1)S(1)}, u32[]{:S(2)}, u32[]{:S(2)}) collective-permute-start(bf16[12,128,128]{2,1,0:T(8,128)(2,1)S(1)} %pad_maximum_fusion), channel_id=1, source_target_pairs={{0,2},{1,3},{2,0},{3,1},{4,6},{5,7},{6,4},{7,5},{8,10},{9,11},{10,... | collective-permute-start | bytes 1179656 | tf_op jit(solution)/shard_map/ppermute | solution.py:24
  93.9 7.7 %collective-permute-start.7 = (bf16[36,128,128]{2,1,0:T(8,128)(2,1)S(1)}, bf16[36,128,128]{2,1,0:T(8,128)(2,1)S(1)}, u32[]{:S(2)}, u32[]{:S(2)}) collective-permute-start(bf16[36,128,128]{2,1,0:T(8,128)(2,1)S(1)} %constant_dynamic-update-slice_fusion.mine_ref), channel_id=1, source_target_pairs={{0,1},{1,0},{2,3},{3,2},{4,5},{5,4},{6,7},{7,6},{8,9},{9,8},{10,11... | collective-permute-start | bytes 3538952 | tf_op jit(solution)/shard_map/ppermute | solution.py:24
